TPU v7x, 256 devices: a whole 4x4x8 slice. The times are simulated.
256 devices in a mesh: tm: 64 (over y, z, core), region: 4 (over x).
Axes of the slice: x: 4, y: 4, z: 8, core: 2. Of those that a mesh axis runs over, the one named last changes fastest.
Arguments:
- covariates: bfloat16 [8, 8192, 256], P('region', 'tm'), may hold values from -4 to 4
- observed: float32 [8, 8192, 256], P('region', 'tm'), may hold values from -40 to 40
- input_weight: bfloat16 [256, 256], replicated, may hold values from -0.375 to 0.375
- filter_weight: bfloat16 [3, 512, 512], replicated, may hold values from -0.25 to 0.25
- mixing_weight: bfloat16 [3, 256, 256], replicated, may hold values from -0.375 to 0.375
- output_weight: bfloat16 [256, 4096], replicated, may hold values from -0.375 to 0.375
Outputs:
- covariate_grad: bfloat16 [8, 8192, 256], P('region', 'tm')
- input_grad: bfloat16 [256, 256], P('tm')
- filter_grad: bfloat16 [3, 512, 512], P(None, 'tm')
- mixing_grad: bfloat16 [3, 256, 256], P(None, 'tm')
- output_grad: bfloat16 [256, 4096], P('tm')
All inputs are finite; a program needn't handle non-finite values.
Results may differ from a plain program's by a relative error of at most 0.022.
Values may be sent and summed in bfloat16 or wider, within the bound.
No kernel may reach another device: no remote copies, remote signals or barrier semaphores. Data moves between devices by JAX's collectives and lax.ppermute only.
A program may use at most 64 MiB of HBM per device.

v0:
```python
import jax
import jax.numpy as jnp
from jax import lax
from jax.sharding import PartitionSpec as P

epsilon = 1e-05


def passed_along(block, axis, distance):
    devices = range(lax.axis_size(axis))
    route = [(i - distance, i) for i in devices if i - distance in devices]
    return lax.ppermute(block, axis, route)


def energy(predicted, observed, scenarios):
    node_count = observed.shape[-1]
    scenario_vals = predicted.reshape(predicted.shape[:-1] + (scenarios, node_count))
    gram_matrix = jnp.einsum(
        "...sn,...rn->...sr", scenario_vals, scenario_vals, precision=lax.Precision.HIGHEST
    )
    against = jnp.einsum(
        "...sn,...n->...s", scenario_vals, observed, precision=lax.Precision.HIGHEST
    )
    own_sq = jnp.diagonal(gram_matrix, axis1=-2, axis2=-1)
    target = jnp.sum(observed * observed, axis=-1)
    to_target = jnp.sqrt((own_sq - 2.0 * against + target[..., None]) / node_count + epsilon)
    off_diag = 1.0 - jnp.eye(scenarios, dtype=jnp.float32)
    pair_sq = (own_sq[..., :, None] + own_sq[..., None, :] - 2.0 * gram_matrix) / node_count
    between = jnp.sqrt(pair_sq * off_diag + epsilon) * off_diag
    return jnp.mean(to_target, axis=-1) - jnp.sum(between, axis=(-2, -1)) / (
        2.0 * scenarios * (scenarios - 1)
    )


def layer_forward(hidden, delayed, w_filter, w_mixing):
    channels = hidden.shape[-1]
    joined = jnp.concatenate([delayed, hidden], axis=-1)
    preact = jnp.dot(joined, w_filter, preferred_element_type=jnp.float32)
    gated = (jnp.tanh(preact[..., :channels]) * jax.nn.sigmoid(preact[..., channels:])).astype(
        jnp.bfloat16
    )
    result = (
        hidden.astype(jnp.float32) + jnp.dot(gated, w_mixing, preferred_element_type=jnp.float32)
    ).astype(jnp.bfloat16)
    return (result, (joined, preact, gated))


def layer_backward(grad_out, stored_layer, w_filter, w_mixing):
    joined, preact, gated = stored_layer
    channels = gated.shape[-1]
    upstream = grad_out.astype(jnp.float32)
    grad_mixing = jnp.einsum("btc,btd->cd", gated, upstream, preferred_element_type=jnp.float32)
    gated_cot = jnp.dot(upstream, w_mixing.T, preferred_element_type=jnp.float32).astype(
        jnp.bfloat16
    )
    grad_gated = lax.optimization_barrier(gated_cot).astype(jnp.float32)
    filter_act = jnp.tanh(preact[..., :channels])
    gate_act = jax.nn.sigmoid(preact[..., channels:])
    grad_preact = jnp.concatenate(
        [
            grad_gated * gate_act * (1.0 - filter_act * filter_act),
            grad_gated * filter_act * gate_act * (1.0 - gate_act),
        ],
        axis=-1,
    )
    grad_filter = jnp.einsum("btk,btj->kj", joined, grad_preact, preferred_element_type=jnp.float32)
    grad_joined = jnp.dot(grad_preact, w_filter.T, preferred_element_type=jnp.float32).astype(
        jnp.bfloat16
    )
    return (
        grad_joined[..., :channels],
        grad_joined[..., channels:],
        grad_out,
        grad_filter,
        grad_mixing,
    )


def per_device(covariates, observed, input_weight, filter_weight, mixing_weight, output_weight):
    batch_seqs, row_count, node_count = covariates.shape
    layer_total = filter_weight.shape[0]
    channels = mixing_weight.shape[1]
    scenarios = output_weight.shape[1] // node_count
    length = row_count * lax.axis_size("tm")
    local_sq = jnp.sum(observed * observed, axis=(1, 2))
    total_sq = lax.psum(local_sq, "tm")
    inv_scale = 1.0 / jnp.sqrt(total_sq / (length * node_count) + epsilon)
    hidden = jnp.dot(covariates, input_weight, preferred_element_type=jnp.float32).astype(
        jnp.bfloat16
    )
    stored = []
    for layer_no in range(layer_total):
        dilation = 2**layer_no
        incoming = passed_along(hidden[:, row_count - dilation :, :], "tm", 1)
        delayed = jnp.concatenate([incoming, hidden[:, : row_count - dilation, :]], axis=1)
        hidden, stored_layer = layer_forward(
            hidden, delayed, filter_weight[layer_no], mixing_weight[layer_no]
        )
        stored.append(stored_layer)
    predicted = jnp.dot(hidden, output_weight, preferred_element_type=jnp.float32)

    def scoring(values):
        return jnp.sum(energy(values, observed, scenarios) * inv_scale[:, None])

    _, pull_back = jax.vjp(scoring, predicted)
    (grad_pred,) = pull_back(jnp.ones((), jnp.float32))
    grad_output = jnp.einsum("btc,btj->cj", hidden, grad_pred, preferred_element_type=jnp.float32)
    grad_last = jnp.dot(grad_pred, output_weight.T, preferred_element_type=jnp.float32).astype(
        jnp.bfloat16
    )
    grad_hidden = grad_last
    filter_parts = [None] * layer_total
    mixing_parts = [None] * layer_total
    for layer_no in reversed(range(layer_total)):
        dilation = 2**layer_no
        grad_past, grad_now, grad_resid, grad_filter, grad_mixing = layer_backward(
            grad_hidden, stored[layer_no], filter_weight[layer_no], mixing_weight[layer_no]
        )
        extent = grad_past.shape[1]
        inside = jnp.concatenate(
            [grad_past[:, dilation:, :], jnp.zeros((batch_seqs, dilation, channels), jnp.bfloat16)],
            axis=1,
        )
        grad_hidden = grad_resid + grad_now + inside
        returned = passed_along(grad_past[:, :dilation, :], "tm", -1)
        grad_hidden = grad_hidden + jnp.concatenate(
            [jnp.zeros((batch_seqs, extent - dilation, channels), jnp.bfloat16), returned], axis=1
        )
        filter_parts[layer_no] = grad_filter
        mixing_parts[layer_no] = grad_mixing
    grad_input = jnp.einsum(
        "btn,btc->nc", covariates, grad_hidden, preferred_element_type=jnp.float32
    )
    covariate_grad = jnp.dot(
        grad_hidden, input_weight.T, preferred_element_type=jnp.float32
    ).astype(jnp.bfloat16)
    grad_filters = jnp.stack(filter_parts)
    grad_mixings = jnp.stack(mixing_parts)
    shares = (
        lax.psum_scatter(grad_input, "tm", scatter_dimension=0, tiled=True),
        lax.psum_scatter(grad_filters, "tm", scatter_dimension=1, tiled=True),
        lax.psum_scatter(grad_mixings, "tm", scatter_dimension=1, tiled=True),
        lax.psum_scatter(grad_output, "tm", scatter_dimension=0, tiled=True),
    )
    shares = (
        lax.psum(shares[0].astype(jnp.bfloat16), "region").astype(jnp.float32),
        lax.psum(shares[1].astype(jnp.bfloat16), "region").astype(jnp.float32),
        lax.psum(shares[2].astype(jnp.bfloat16), "region").astype(jnp.float32),
        lax.psum(shares[3].astype(jnp.bfloat16), "region").astype(jnp.float32),
    )
    shares = tuple((piece.astype(jnp.bfloat16) for piece in shares))
    return (covariate_grad, shares[0], shares[1], shares[2], shares[3])


def solution(mesh):
    placed = (P("region", "tm", None), P("region", "tm", None), P(), P(), P(), P())
    return jax.shard_map(
        per_device,
        mesh=mesh,
        in_specs=placed,
        out_specs=(
            P("region", "tm", None),
            P("tm", None),
            P(None, "tm", None),
            P(None, "tm", None),
            P("tm", None),
        ),
        check_vma=False,
    )
```

profile of v0, /device:TPU:8, one launch (start us, length us, event | category | flops | bytes accessed | tf_op | source)
XLA Modules:
  0.0 587.4 jit_solution(2315299154174542685)
XLA Ops:
  7.2 1.3 convolution_convert_fusion.7
  8.5 1.9 collective-permute-start
  10.5 1.7 multiply_reduce_fusion.1
  12.2 109.8 %psum.35 = f32[2]{0:T(128)S(1)} all-reduce(f32[2]{0:T(128)S(1)} %get-tuple-element.28), channel_id=1, replica_groups=mesh['tm'=64,'region'=4] {'tm'}, use_global_device_ids=true, to_apply=%region_2.3 | all-reduce | flops 2 | bytes 16 | tf_op jit(solution)/shard_map/psum | solution.py:86
  122.0 0.6 broadcast_multiply_fusion.1
  122.6 0.6 convert_subtract_fusion
  123.2 1.4 fusion.27
  124.8 1.1 fusion.14
  125.9 1.9 collective-permute-start.1
  127.8 0.5 fusion.85
  128.4 4.6 collective-permute-done.1
  132.9 0.6 copy-done.28
  134.2 1.9 collective-permute-start.2
  136.1 0.5 fusion.84
  136.6 4.6 collective-permute-done.2
  141.2 0.3 fusion.21
  141.8 0.5 copy-done.7
  142.3 0.6 copy-done.17
  143.2 0.7 fusion.12
  143.9 1.7 copy.97
  145.7 1.9 copy-done.1
  147.6 6.3 %fusion.6 = f32[2,128,16,16]{3,2,1,0:T(8,128)} fusion(f32[2,128,16,256]{3,2,1,0:T(8,128)S(1)} %bitcast.162), kind=kOutput, calls=%fused_computation.9 | convolution fusion | flops 201326592 | bytes 4456448 | tf_op jit(solution)/shard_map/jvp(...sn,...rn->...sr)/dot_general | solution.py:18
  153.9 3.2 copy.60
  157.2 2.3 copy.63
  159.5 1.7 gather_fusion
  161.1 0.6 copy.107
  161.8 6.5 %fusion.4 = f32[2,128,1,16]{3,2,1,0:T(1,128)} fusion(f32[2,128,256,1]{2,1,0,3:T(8,128)S(1)} %bitcast.167, f32[2,128,16,256]{3,2,1,0:T(8,128)} %bitcast.163), kind=kOutput, calls=%fused_computation.7 | convolution fusion | flops 12582912 | bytes 4472832 | tf_op jit(solution)/shard_map/jvp(...sn,...n->...s)/dot_general | solution.py:21
  168.2 1.6 copy.82
  169.8 1.0 fusion.99
  170.8 1.4 negate_multiply_fusion.1
  172.4 1.6 scatter_fusion
  174.1 2.1 copy.71
  176.3 6.9 %fusion = f32[2,128,16,256]{3,2,1,0:T(8,128)S(1)} fusion(f32[2,128,16,16]{3,2,1,0:T(8,128)} %copy.71, f32[2,128,16,256]{3,2,1,0:T(8,128)} %bitcast.164), kind=kOutput, calls=%fused_computation.3 | convolution fusion | flops 201326592 | bytes 8650752 | tf_op jit(solution)/shard_map/transpose(jvp(...sn,...rn->...sr))/dot_general | solution.py:18
  183.2 5.7 add_add_fusion
  188.9 4.2 reshape.36
  193.1 2.5 fusion.17
  196.1 0.3 convolution_convert_fusion.2
  196.4 1.9 collective-permute-start.3
  198.3 0.3 convolution_bitcast_fusion.1
  198.7 0.9 collective-permute-done.3
  200.1 0.3 convolution_convert_fusion.1
  200.5 5.7 collective-permute-start.4
  206.2 0.3 convolution_bitcast_fusion.2
  206.6 0.9 collective-permute-done.4
  207.9 0.3 convolution_bitcast_fusion.3
  208.3 0.3 copy-done.20
  208.6 2.0 pad_maximum_fusion
  210.6 0.6 copy-done.32
  211.2 0.6 dynamic-slice
  212.5 4.3 convolution_bitcast_fusion
  217.3 1.4 convolution_convert_fusion
  218.8 5.7 collective-permute-start.5
  224.8 0.9 collective-permute-done.5
  226.1 264.1 %all-reduce.15 = (bf16[256,256]{0,1:T(8,128)(2,1)S(1)}, bf16[3,256,256]{2,1,0:T(8,128)(2,1)}, bf16[256,4096]{1,0:T(8,128)(2,1)}) all-reduce(f32[256,256]{0,1:T(8,128)S(1)} %convolution_bitcast_fusion.7, f32[3,256,256]{2,1,0:T(8,128)S(1)} %pad_maximum_fusion.1, ...), channel_id=2, replica_groups=mesh['tm'=64,'region'=4] {'tm'}, use_global_device_ids=true, to_apply=%region_6.7.clone | all-reduce | flops 1310720 | bytes 7864320
  490.2 1.3 dynamic-slice_convert_fusion.2
  491.6 0.7 dynamic-slice_convert_fusion
  492.3 1.5 dynamic-slice_convert_fusion.1
  493.7 1.4 convert_element_type.120
  495.2 0.9 convolution_convert_fusion.3
  496.1 79.0 %all-reduce.14.cloned.1.call-done = (bf16[4,256]{0,1:T(8,128)(2,1)}, bf16[3,8,512]{2,1,0:T(8,128)(2,1)}, bf16[3,4,256]{2,1,0:T(4,128)(2,1)}, bf16[4,4096]{1,0:T(4,128)(2,1)}) async-done(((bf16[4,256]{0,1:T(8,128)(2,1)}, bf16[3,8,512]{2,1,0:T(8,128)(2,1)}, bf16[3,4,256]{2,1,0:T(4,128)(2,1)}, bf16[4,4096]{1,0:T(4,128)(2,1)}), (bf16[4,256]{0,1:T(8,128)(2,1)}, bf16[3,8,512]{2,1,0:T(8,128)(2,1)}, ...) | async-done | bytes 65552 | tf_op jit(solution)/shard_map/psum | solution.py:146
  575.0 1.5 copy.80
  576.6 1.3 copy.119
  577.9 1.3 copy.120
  579.2 1.4 copy.121
  (98 shorter events, 4.1 us)
Async XLA Ops:
  7.2 136.0 %copy-start = (bf16[256,4096]{1,0:T(8,128)(2,1)S(1)}, bf16[256,4096]{1,0:T(8,128)(2,1)}, u32[]{:S(2)}) copy-start(bf16[256,4096]{1,0:T(8,128)(2,1)} %param.11) | copy-start | bytes 6291460
  7.2 486.6 %reduce-scatter.4.cloned.1.call-start = ((), (), s32[]{:S(2)}) async-start(), calls=%async_computation.1 | async-start | bytes 3194880 | tf_op jit(solution)/shard_map/reduce_scatter | solution.py:141
  8.5 114.7 %collective-permute-start = (bf16[2,1,256]{2,1,0:T(2,128)(2,1)S(1)}, bf16[2,1,256]{2,1,0:T(2,128)(2,1)S(1)}, u32[]{:S(2)}, u32[]{:S(2)}) collective-permute-start(bf16[2,1,256]{2,1,0:T(2,128)(2,1)S(1)} %slice.133), channel_id=1, source_target_pairs={{0,4},{4,8},{8,12},{12,16},{16,20},{20,24},{24,28},{28,32},{32,36}... | collective-permute-start | bytes 3080 | tf_op jit(solution)/shard_map/ppermute | solution.py:12
  122.0 11.5 %copy-start.30 = (bf16[3,512,512]{2,1,0:T(8,128)(2,1)S(1)}, bf16[3,512,512]{2,1,0:T(8,128)(2,1)}, u32[]{:S(2)}) copy-start(bf16[3,512,512]{2,1,0:T(8,128)(2,1)} %param.9) | copy-start | bytes 4718596
  123.2 1.4 copy-start.26
  123.2 10.7 %copy-start.9 = (bf16[3,256,256]{2,1,0:T(8,128)(2,1)S(1)}, bf16[3,256,256]{2,1,0:T(8,128)(2,1)}, u32[]{:S(2)}) copy-start(bf16[3,256,256]{2,1,0:T(8,128)(2,1)} %param.10) | copy-start | bytes 1179652
  124.7 8.2 %copy-start.13 = (bf16[2,128,256]{2,1,0:T(8,128)(2,1)}, bf16[2,128,256]{2,1,0:T(8,128)(2,1)S(1)}, u32[]{:S(2)}) copy-start(bf16[2,128,256]{2,1,0:T(8,128)(2,1)S(1)} %multiply_convert_fusion.2) | copy-start | bytes 393220
  125.9 7.0 %collective-permute-start.1 = (bf16[2,2,256]{2,1,0:T(2,128)(2,1)S(1)}, bf16[2,2,256]{2,1,0:T(2,128)(2,1)S(1)}, u32[]{:S(2)}, u32[]{:S(2)}) collective-permute-start(bf16[2,2,256]{2,1,0:T(2,128)(2,1)S(1)} %slice.137), channel_id=1, source_target_pairs={{0,4},{4,8},{8,12},{12,16},{16,20},{20,24},{24,28},{28,32},{32,36}... | collective-permute-start | bytes 6152 | tf_op jit(solution)/shard_map/ppermute | solution.py:12
  132.9 0.6 copy-start.28
  133.8 7.8 %copy-start.5 = (f32[2,128,512]{2,1,0:T(8,128)}, f32[2,128,512]{2,1,0:T(8,128)S(1)}, u32[]{:S(2)}) copy-start(f32[2,128,512]{2,1,0:T(8,128)S(1)} %fusion.24) | copy-start | bytes 1572868
  134.0 7.3 %copy-start.15 = (bf16[2,128,256]{2,1,0:T(8,128)(2,1)}, bf16[2,128,256]{2,1,0:T(8,128)(2,1)S(1)}, u32[]{:S(2)}) copy-start(bf16[2,128,256]{2,1,0:T(8,128)(2,1)S(1)} %multiply_convert_fusion.1) | copy-start | bytes 393220
  134.2 7.0 %collective-permute-start.2 = (bf16[2,4,256]{2,1,0:T(4,128)(2,1)S(1)}, bf16[2,4,256]{2,1,0:T(4,128)(2,1)S(1)}, u32[]{:S(2)}, u32[]{:S(2)}) collective-permute-start(bf16[2,4,256]{2,1,0:T(4,128)(2,1)S(1)} %slice.141), channel_id=1, source_target_pairs={{0,4},{4,8},{8,12},{12,16},{16,20},{20,24},{24,28},{28,32},{32,36}... | collective-permute-start | bytes 12296 | tf_op jit(solution)/shard_map/ppermute | solution.py:12
  141.2 0.6 copy-start.24
  141.5 0.8 copy-start.7
  142.3 0.6 copy-start.17
  143.2 0.7 copy-start.11
  145.7 2.0 copy-start.1
  153.9 7.8 %copy-start.4 = (f32[2,128,256]{2,1,0:T(8,128)S(1)}, f32[2,128,256]{2,1,0:T(8,128)}, u32[]{:S(2)}) copy-start(f32[2,128,256]{2,1,0:T(8,128)} %param.7) | copy-start | bytes 786436
  174.1 2.1 copy-start.23
  176.3 6.9 %copy-start.2 = (f32[32,8,16,256]{3,2,1,0:T(8,128)S(1)}, f32[32,8,16,256]{3,2,1,0:T(8,128)}, u32[]{:S(2)}) copy-start(f32[32,8,16,256]{3,2,1,0:T(8,128)} %copy-done.1) | copy-start | bytes 12582916
  176.3 6.9 %copy-start.3 = (f32[2,128,16,16]{3,2,1,0:T(8,128)S(1)}, f32[2,128,16,16]{3,2,1,0:T(8,128)}, u32[]{:S(2)}) copy-start(f32[2,128,16,16]{3,2,1,0:T(8,128)} %copy.71) | copy-start | bytes 786436
  193.1 2.5 copy-start.10
  193.1 2.7 copy-start.8
  193.1 2.9 copy-start.31
  195.6 2.7 copy-start.25
  196.0 3.9 copy-start.6
  196.4 3.2 collective-permute-start.3
  198.7 7.5 %copy-start.29 = (bf16[2,2,256]{2,1,0:T(2,128)(2,1)S(1)}, bf16[2,2,256]{2,1,0:T(2,128)(2,1)}, u32[]{:S(2)}) copy-start(bf16[2,2,256]{2,1,0:T(2,128)(2,1)} %copy-done.28) | copy-start | bytes 6148
  200.4 7.5 %copy-start.27 = (bf16[2,1,256]{2,1,0:T(2,128)(2,1)S(1)}, bf16[2,1,256]{2,1,0:T(2,128)(2,1)}, u32[]{:S(2)}) copy-start(bf16[2,1,256]{2,1,0:T(2,128)(2,1)} %copy-done.26) | copy-start | bytes 3076
  200.5 7.0 %collective-permute-start.4 = (bf16[2,2,256]{2,1,0:T(2,128)(2,1)S(1)}, bf16[2,2,256]{2,1,0:T(2,128)(2,1)S(1)}, u32[]{:S(2)}, u32[]{:S(2)}) collective-permute-start(bf16[2,2,256]{2,1,0:T(2,128)(2,1)S(1)} %slice.150), channel_id=1, source_target_pairs={{4,0},{8,4},{12,8},{16,12},{20,16},{24,20},{28,24},{32,28},{36,32}... | collective-permute-start | bytes 6152 | tf_op jit(solution)/shard_map/ppermute | solution.py:12
  207.9 0.7 copy-start.20
  210.6 0.7 copy-start.32
  210.6 1.9 copy-start.12
  210.6 364.5 %all-reduce.14.cloned.1.call-start = ((), (), s32[]{:S(2)}) async-start(), calls=%async_computation.2 | async-start | bytes 258048 | tf_op jit(solution)/shard_map/psum | solution.py:146
  212.5 4.4 copy-start.18
  212.5 4.6 copy-start.16
  212.5 4.8 copy-start.21
  216.9 7.6 %copy-start.14 = (bf16[2,128,256]{2,1,0:T(8,128)(2,1)S(1)}, bf16[2,128,256]{2,1,0:T(8,128)(2,1)}, u32[]{:S(2)}) copy-start(bf16[2,128,256]{2,1,0:T(8,128)(2,1)} %copy-done.13) | copy-start | bytes 393220
  217.3 8.5 %copy-start.22 = (bf16[2,128,256]{2,1,0:T(8,128)(2,1)S(1)}, bf16[2,128,256]{2,1,0:T(8,128)(2,1)}, u32[]{:S(2)}) copy-start(bf16[2,128,256]{2,1,0:T(8,128)(2,1)} %param.6) | copy-start | bytes 393220
  218.8 7.0 %collective-permute-start.5 = (bf16[2,1,256]{2,1,0:T(2,128)(2,1)S(1)}, bf16[2,1,256]{2,1,0:T(2,128)(2,1)S(1)}, u32[]{:S(2)}, u32[]{:S(2)}) collective-permute-start(bf16[2,1,256]{2,1,0:T(2,128)(2,1)S(1)} %slice.153), channel_id=1, source_target_pairs={{4,0},{8,4},{12,8},{16,12},{20,16},{24,20},{28,24},{32,28},{36,32}... | collective-permute-start | bytes 3080 | tf_op jit(solution)/shard_map/ppermute | solution.py:12
  226.1 269.1 %copy-start.19 = (bf16[256,256]{1,0:T(8,128)(2,1)S(1)}, bf16[256,256]{1,0:T(8,128)(2,1)}, u32[]{:S(2)}) copy-start(bf16[256,256]{1,0:T(8,128)(2,1)} %param.8) | copy-start | bytes 393220
Sparse Core Ops, SparseCore 0:
  210.7 148.8 reduce-scatter.3
  495.3 79.7 all-reduce.13
where the time goes:
time: 589 us; the launch traced here: 587 us
  blocking collectives  374 us (63%)
  waiting for transfers between devices  91 us (15%)
  matrix products  43.1 us (7%)
  local copies, waits for them, and re-layouts  32.3 us (5%)
  starting transfers between devices  19.2 us (3%)
  between operations  15.4 us (3%)
  other arithmetic  12.4 us (2%)
    unnamed x1, blocking collectives  264 us
    psum x1, blocking collectives, per_device(): total_sq = lax.psum(local_sq, 'tm')  110 us
    psum x1, waiting for transfers between devices, per_device(): lax.psum(shares[0].astype(jnp.bfloat16), 'region').astype(jnp.float32)  79 us
    ppermute x6, starting transfers between devices, passed_along(): return lax.ppermute(block, axis, route)  19.1 us
    dot_general x3, matrix products, energy(): jnp.einsum('...sn,...rn->...sr', scenario_vals, scenario_vals, precision=...  18.9 us
    unnamed x72, local copies, waits for them, and re-layouts  12.7 us
    ppermute x6, waiting for transfers between devices, passed_along(): return lax.ppermute(block, axis, route)  11.9 us
  transfers between devices with their start and end apart: 8, of which 6 were waited for; matrix products, arithmetic and copies ran while one was open for 3% of the time, Pallas kernels for 0%

commit v1 on v0

--- a/solution.py
+++ b/solution.py
@@ -4,6 +4,10 @@
 from jax.sharding import PartitionSpec as P
 
 epsilon = 1e-05
+
+
+def apply_frames(matrix):
+    return jnp.sum(jax.lax.all_gather(matrix, axis_name="region"), axis=0)
 
 
 def passed_along(block, axis, distance):
@@ -143,7 +147,7 @@
         lax.psum_scatter(grad_output, "tm", scatter_dimension=0, tiled=True),
     )
     shares = (
-        lax.psum(shares[0].astype(jnp.bfloat16), "region").astype(jnp.float32),
+        apply_frames(shares[0].astype(jnp.bfloat16)).astype(jnp.float32),
         lax.psum(shares[1].astype(jnp.bfloat16), "region").astype(jnp.float32),
         lax.psum(shares[2].astype(jnp.bfloat16), "region").astype(jnp.float32),
         lax.psum(shares[3].astype(jnp.bfloat16), "region").astype(jnp.float32),

time: 589 us -> 569 us (0.966)
  the two profiles are of different devices: /device:TPU:8 before, /device:TPU:4 now
where the time goes in v1:
time: 569 us; the launch traced here: 568 us
  blocking collectives  454 us (80%)
  matrix products  43.1 us (8%)
  local copies, waits for them, and re-layouts  25.1 us (4%)
  between operations  15.4 us (3%)
  other arithmetic  12.5 us (2%)
  starting transfers between devices  9.19 us (2%)
  waiting for transfers between devices  8.41 us (1%)
    unnamed x1, blocking collectives  296 us
    psum x1, blocking collectives, per_device(): total_sq = lax.psum(local_sq, 'tm')  131 us
    dot_general x3, matrix products, energy(): jnp.einsum('...sn,...rn->...sr', scenario_vals, scenario_vals, precision=...  18.9 us
    psum x1, blocking collectives, per_device(): lax.psum(shares[1].astype(jnp.bfloat16), 'region').astype(jnp.float32)  16.5 us
  transfers between devices with their start and end apart: 7, of which 5 were waited for; matrix products, arithmetic and copies ran while one was open for 3% of the time, Pallas kernels for 0%

profile of v1, /device:TPU:4, one launch (start us, length us, event | category | flops | bytes accessed | tf_op | source)
XLA Modules:
  0.0 567.5 jit_solution(14147904439924340539)
XLA Ops:
  7.2 1.3 convolution_convert_fusion.7
  8.5 1.7 collective-permute-start
  10.3 1.7 multiply_reduce_fusion.1
  12.0 131.3 %psum.28 = f32[2]{0:T(128)S(1)} all-reduce(f32[2]{0:T(128)S(1)} %get-tuple-element.18), channel_id=1, replica_groups=mesh['tm'=64,'region'=4] {'tm'}, use_global_device_ids=true, to_apply=%region_2.3 | all-reduce | flops 2 | bytes 16 | tf_op jit(solution)/shard_map/psum | solution.py:90
  143.3 0.6 broadcast_multiply_fusion.1
  143.9 0.6 convert_subtract_fusion
  144.5 1.4 fusion.27
  146.1 1.1 fusion.14
  147.2 1.3 collective-permute-start.1
  148.5 0.5 fusion.86
  149.1 0.3 collective-permute-done.1
  149.3 0.6 copy-done.28
  149.9 0.3 fusion.24
  150.6 2.2 collective-permute-start.2
  152.8 0.6 fusion.85
  153.4 0.2 collective-permute-done.2
  153.7 0.3 fusion.21
  154.2 0.5 copy-done.7
  154.8 0.6 copy-done.17
  155.6 0.7 fusion.12
  156.3 1.7 copy.100
  158.1 1.9 copy-done.1
  160.0 6.3 %fusion.6 = f32[2,128,16,16]{3,2,1,0:T(8,128)} fusion(f32[2,128,16,256]{3,2,1,0:T(8,128)S(1)} %bitcast.164), kind=kOutput, calls=%fused_computation.9 | convolution fusion | flops 201326592 | bytes 4456448 | tf_op jit(solution)/shard_map/jvp(...sn,...rn->...sr)/dot_general | solution.py:22
  166.3 3.2 copy.60
  169.5 2.3 copy.63
  171.8 1.7 gather_fusion
  173.5 0.6 copy.110
  174.1 6.5 %fusion.4 = f32[2,128,1,16]{3,2,1,0:T(1,128)} fusion(f32[2,128,256,1]{2,1,0,3:T(8,128)S(1)} %bitcast.169, f32[2,128,16,256]{3,2,1,0:T(8,128)} %bitcast.165), kind=kOutput, calls=%fused_computation.7 | convolution fusion | flops 12582912 | bytes 4472832 | tf_op jit(solution)/shard_map/jvp(...sn,...n->...s)/dot_general | solution.py:25
  180.6 1.6 copy.84
  182.2 1.0 fusion.100
  183.2 1.4 negate_multiply_fusion.1
  184.8 1.6 scatter_fusion
  186.5 2.1 copy.71
  188.7 6.9 %fusion = f32[2,128,16,256]{3,2,1,0:T(8,128)S(1)} fusion(f32[2,128,16,16]{3,2,1,0:T(8,128)} %copy.71, f32[2,128,16,256]{3,2,1,0:T(8,128)} %bitcast.166), kind=kOutput, calls=%fused_computation.3 | convolution fusion | flops 201326592 | bytes 8650752 | tf_op jit(solution)/shard_map/transpose(jvp(...sn,...rn->...sr))/dot_general | solution.py:22
  195.6 5.7 %add_add_fusion = bf16[2,128,16,256]{3,2,1,0:T(8,128)(2,1)} fusion(f32[2,128,16,256]{3,2,1,0:T(8,128)S(1)} %fusion, f32[2,128,16,16]{3,2,1,0:T(8,128)S(1)} %copy-done.3, f32[2,128,256]{2,1,0:T(8,128)S(1)} %copy-done.4, f32[2,128,16]{2,1,0:T(8,128)S(1)} %copy.62, f32[2,128,16,256]{3,2,1,0:T(8,128)S(1)} %bitcast.167), kind=kOutput, calls=%fused_computation.11 | convolution fusion | flops 205520896 | bytes 11026432 | tf_op jit(solution)/shard_map/transpose(jvp(...sn,...rn->...sr))/dot_general | solution.py:22
  201.3 4.2 reshape.36
  205.5 2.5 fusion.17
  208.0 0.2 convolution_convert_fusion.6
  208.4 0.3 convolution_convert_fusion.2
  208.8 1.3 collective-permute-start.3
  210.1 0.3 convolution_bitcast_fusion.1
  210.5 1.4 collective-permute-done.3
  212.3 0.3 convolution_convert_fusion.1
  212.7 1.3 collective-permute-start.4
  214.0 0.3 convolution_bitcast_fusion.2
  214.4 3.2 collective-permute-done.4
  218.0 0.3 convolution_bitcast_fusion.3
  218.4 0.3 copy-done.20
  218.7 2.0 pad_maximum_fusion
  220.7 0.6 copy-done.32
  221.4 0.6 dynamic-slice
  222.6 4.3 convolution_bitcast_fusion
  227.4 1.4 convolution_convert_fusion
  228.9 1.3 collective-permute-start.5
  230.5 3.3 collective-permute-done.5
  233.8 0.2 convolution_bitcast_fusion.7
  234.1 295.9 %all-reduce.12 = (bf16[256,256]{0,1:T(8,128)(2,1)S(1)}, bf16[3,256,256]{2,1,0:T(8,128)(2,1)}, bf16[256,4096]{1,0:T(8,128)(2,1)}) all-reduce(f32[256,256]{0,1:T(8,128)S(1)} %convolution_bitcast_fusion.7, f32[3,256,256]{2,1,0:T(8,128)S(1)} %pad_maximum_fusion.1, ...), channel_id=3, replica_groups=mesh['tm'=64,'region'=4] {'tm'}, use_global_device_ids=true, to_apply=%region_6.7.clone | all-reduce | flops 1310720 | bytes 7864320
  530.2 10.1 %all-gather.1 = bf16[4,4,256]{2,1,0:T(4,128)(2,1)S(1)} all-gather(bf16[1,4,256]{2,1,0:T(4,128)(2,1)S(1)} %copy.73), channel_id=2, replica_groups=mesh['tm'=64,'region'=4] {'region'}, dimensions={0}, use_global_device_ids=true | all-gather | bytes 10240 | tf_op jit(solution)/shard_map/all_gather | solution.py:10
  540.3 0.6 reduce_sum.60
  540.9 0.7 dynamic-slice_convert_fusion.2
  541.6 0.9 convolution_convert_fusion.3
  542.5 0.9 dynamic-slice_convert_fusion.1
  543.4 0.8 convert_element_type.122
  544.2 16.5 %all-reduce.10 = (bf16[3,8,512]{2,1,0:T(8,128)(2,1)}, bf16[3,4,256]{2,1,0:T(4,128)(2,1)}, bf16[4,4096]{1,0:T(4,128)(2,1)}) all-reduce(bf16[3,8,512]{2,1,0:T(8,128)(2,1)S(1)} %convert_element_type.122, bf16[3,4,256]{2,1,0:T(4,128)(2,1)S(1)} %dynamic-slice_convert_fusion.2, ...), channel_id=1, replica_groups=mesh['tm'=64,'region'=4] {'region'}, use_global_device_ids=true, to_apply=%region_9.10 | all-reduce | flops 31744 | bytes 126976 | tf_op jit(solution)/shard_map/psum | solution.py:151
  (95 shorter events, 3.5 us)
Async XLA Ops:
  7.2 148.4 %copy-start = (bf16[256,4096]{1,0:T(8,128)(2,1)S(1)}, bf16[256,4096]{1,0:T(8,128)(2,1)}, u32[]{:S(2)}) copy-start(bf16[256,4096]{1,0:T(8,128)(2,1)} %param.11) | copy-start | bytes 6291460
  7.2 536.2 %reduce-scatter.4.cloned.1.call-start = ((), (), s32[]{:S(2)}) async-start(), calls=%async_computation.1 | async-start | bytes 3194880 | tf_op jit(solution)/shard_map/reduce_scatter | solution.py:145
  8.5 136.0 %collective-permute-start = (bf16[2,1,256]{2,1,0:T(2,128)(2,1)S(1)}, bf16[2,1,256]{2,1,0:T(2,128)(2,1)S(1)}, u32[]{:S(2)}, u32[]{:S(2)}) collective-permute-start(bf16[2,1,256]{2,1,0:T(2,128)(2,1)S(1)} %slice.133), channel_id=1, source_target_pairs={{0,4},{4,8},{8,12},{12,16},{16,20},{20,24},{24,28},{28,32},{32,36}... | collective-permute-start | bytes 3080 | tf_op jit(solution)/shard_map/ppermute | solution.py:16
  143.3 6.6 %copy-start.30 = (bf16[3,512,512]{2,1,0:T(8,128)(2,1)S(1)}, bf16[3,512,512]{2,1,0:T(8,128)(2,1)}, u32[]{:S(2)}) copy-start(bf16[3,512,512]{2,1,0:T(8,128)(2,1)} %param.9) | copy-start | bytes 4718596
  144.5 1.4 copy-start.26
  144.5 5.8 %copy-start.9 = (bf16[3,256,256]{2,1,0:T(8,128)(2,1)S(1)}, bf16[3,256,256]{2,1,0:T(8,128)(2,1)}, u32[]{:S(2)}) copy-start(bf16[3,256,256]{2,1,0:T(8,128)(2,1)} %param.10) | copy-start | bytes 1179652
  146.1 3.3 copy-start.13
  147.2 2.1 collective-permute-start.1
  149.3 0.6 copy-start.28
  150.2 3.9 copy-start.5
  150.4 3.3 copy-start.15
  150.6 3.1 collective-permute-start.2
  153.6 0.6 copy-start.24
  154.0 0.8 copy-start.7
  154.8 0.6 copy-start.17
  155.6 0.7 copy-start.11
  158.1 1.9 copy-start.1
  166.3 7.8 %copy-start.4 = (f32[2,128,256]{2,1,0:T(8,128)S(1)}, f32[2,128,256]{2,1,0:T(8,128)}, u32[]{:S(2)}) copy-start(f32[2,128,256]{2,1,0:T(8,128)} %param.7) | copy-start | bytes 786436
  186.5 2.1 copy-start.23
  188.7 6.9 %copy-start.2 = (f32[32,8,16,256]{3,2,1,0:T(8,128)S(1)}, f32[32,8,16,256]{3,2,1,0:T(8,128)}, u32[]{:S(2)}) copy-start(f32[32,8,16,256]{3,2,1,0:T(8,128)} %copy-done.1) | copy-start | bytes 12582916
  188.7 6.9 %copy-start.3 = (f32[2,128,16,16]{3,2,1,0:T(8,128)S(1)}, f32[2,128,16,16]{3,2,1,0:T(8,128)}, u32[]{:S(2)}) copy-start(f32[2,128,16,16]{3,2,1,0:T(8,128)} %copy.71) | copy-start | bytes 786436
  205.5 2.5 copy-start.10
  205.5 2.7 copy-start.8
  205.5 2.9 copy-start.31
  208.0 2.1 copy-start.25
  208.4 3.7 copy-start.6
  208.8 3.1 collective-permute-start.3
  210.4 3.5 copy-start.29
  212.6 5.4 copy-start.27
  212.7 4.9 collective-permute-start.4
  218.0 0.7 copy-start.20
  220.7 0.7 copy-start.32
  220.7 1.9 copy-start.12
  222.6 4.3 copy-start.18
  222.6 4.6 copy-start.16
  222.6 4.8 copy-start.21
  226.9 3.2 copy-start.14
  227.4 6.4 %copy-start.22 = (bf16[2,128,256]{2,1,0:T(8,128)(2,1)S(1)}, bf16[2,128,256]{2,1,0:T(8,128)(2,1)}, u32[]{:S(2)}) copy-start(bf16[2,128,256]{2,1,0:T(8,128)(2,1)} %param.6) | copy-start | bytes 393220
  228.9 4.9 collective-permute-start.5
  234.1 307.5 %copy-start.19 = (bf16[256,256]{1,0:T(8,128)(2,1)S(1)}, bf16[256,256]{1,0:T(8,128)(2,1)}, u32[]{:S(2)}) copy-start(bf16[256,256]{1,0:T(8,128)(2,1)} %param.8) | copy-start | bytes 393220
Sparse Core Ops, SparseCore 0:
  220.8 139.8 reduce-scatter.3
